TPU v7x, 256 devices: a whole 4x4x8 slice. The times are simulated.
256 devices in a mesh: blk: 8 (over y, core), sep: 32 (over x, z).
Axes of the slice: x: 4, y: 4, z: 8, core: 2. Of those that a mesh axis runs over, the one named last changes fastest.
Arguments:
- interior_inverse: float32 [8, 32, 1024, 1024], P('blk', 'sep'), as said below
- coupling: float32 [8, 32, 1024, 512], P('blk', 'sep')
- port_matrix: float32 [8, 32, 512, 512], P('blk', 'sep'), as said below
- interior_current: float32 [8, 32, 1024, 128], P('blk', 'sep'), may hold values from -6 to 6
- port_current: float32 [8, 32, 512, 128], P('blk', 'sep'), may hold values from -6 to 6
- port_list: int32 [8, 32, 512], P('blk', 'sep'), may hold values from 0 to 1023, as said below
- spectral_scale: float32 [], replicated, may hold values from 1.5 to 3
Outputs:
- port_voltage: float32 [32, 1024, 128], P('sep', 'blk')
- interior_voltage: float32 [8, 32, 1024, 128], P('blk', 'sep')
Inputs may be any that keep to these rules, and one draw needn't show every extreme that they name: `port_list`: in each block the first 256 entries are distinct, and so are the last ones. Within one separator group, blocks whose b differ by a multiple of 4 name the same sets, and the sets of the first 4 blocks partition the separator's rows, both for the first and for the last halves. `interior_inverse`: symmetric positive definite. Each block's port_matrix minus coupling^T interior_inverse coupling is symmetric positive definite.
All inputs are finite; a program needn't handle non-finite values.
Results may differ from a plain program's by a relative error of at most 0.0001.
Values sent between devices are 32-bit elements; how exact they have to be, the bound alone decides.
No kernel may reach another device: no remote copies, remote signals or barrier semaphores. Data moves between devices by JAX's collectives and lax.ppermute only.
A program may use at most 64 MiB of HBM per device.

v0:
```python
import jax
import jax.numpy as jnp
from jax import lax
from jax.sharding import PartitionSpec as P

SEP_PORTS = 1024
ITERS = 2
DEGREE = 2
HI = lax.Precision.HIGHEST


def shifted(array, axis, by):
    devices = lax.axis_size(axis)
    return lax.ppermute(array, axis, [(i, (i + by) % devices) for i in range(devices)])


def body(
    interior_inverse,
    coupling,
    port_matrix,
    interior_current,
    port_current,
    port_list,
    spectral_scale,
):
    ginv = interior_inverse[0, 0]
    aip = coupling[0, 0]
    app = port_matrix[0, 0]
    inner = interior_current[0, 0]
    outer = port_current[0, 0]
    ports = port_list[0, 0]
    width = aip.shape[1]
    half = width // 2
    lower = ports[:half]
    higher = ports[half:]
    solved = jnp.dot(ginv, jnp.concatenate([aip, inner], axis=1), precision=HI)
    reduced_all = jnp.dot(aip.T, solved, precision=HI)
    schur = app - reduced_all[:, :width]
    reduced = outer - reduced_all[:, width:]

    def spread(owned):
        whole = lax.all_gather(owned, "blk", axis=0, tiled=True)
        after = shifted(whole, "sep", -1)
        return jnp.concatenate([whole[lower], after[higher]], axis=0)

    def split_rows(contrib):
        blank = jnp.zeros((SEP_PORTS, contrib.shape[1]), jnp.float32)
        return (blank.at[lower].add(contrib[:half]), blank.at[higher].add(contrib[half:]))

    def collect(contrib):
        own_part, next_part = split_rows(contrib)
        back = shifted(next_part, "sep", 1)
        return lax.psum_scatter(own_part + back, "blk", scatter_dimension=0, tiled=True)

    diag_column = jnp.diagonal(schur)[:, None]
    own_main, next_main = split_rows(reduced)
    own_diag, next_diag = split_rows(diag_column)
    back_main, back_diag = shifted((next_main, next_diag), "sep", 1)
    rhs, diagonal_sum = (
        lax.psum_scatter(own_main + back_main, "blk", scatter_dimension=0, tiled=True),
        lax.psum_scatter(own_diag + back_diag, "blk", scatter_dimension=0, tiled=True),
    )

    def matvec(vector):
        return collect(jnp.dot(schur, spread(vector), precision=HI))

    def column_sum(left, right):
        return lax.psum(jnp.sum(left * right, axis=0), ("blk", "sep"))

    def precond(residual):
        level = residual / diagonal_sum
        result = level
        for step in range(DEGREE):
            level = level - matvec(level) / (spectral_scale * diagonal_sum)
            result = result + level
        return result

    solution = jnp.zeros_like(rhs)
    residual = rhs
    search = precond(residual)
    direction = search
    inner_rz = column_sum(residual, search)
    for step in range(ITERS):
        image = matvec(direction)
        alpha = inner_rz / column_sum(direction, image)
        solution = solution + alpha * direction
        residual = residual - alpha * image
        if step + 1 < ITERS:
            search = precond(residual)
            newer = column_sum(residual, search)
            direction = search + newer / inner_rz * direction
            inner_rz = newer
    local = spread(solution)
    interior = jnp.dot(ginv, inner - jnp.dot(aip, local, precision=HI), precision=HI)
    return (solution[None], interior[None, None])


def solution(mesh):
    return jax.shard_map(
        body,
        mesh=mesh,
        in_specs=(
            P("blk", "sep", None, None),
            P("blk", "sep", None, None),
            P("blk", "sep", None, None),
            P("blk", "sep", None, None),
            P("blk", "sep", None, None),
            P("blk", "sep", None),
            P(),
        ),
        out_specs=(P("sep", "blk", None), P("blk", "sep", None, None)),
        check_vma=False,
    )
```

profile of v0, /device:TPU:1, one launch (start us, length us, event | category | flops | bytes accessed | tf_op | source)
XLA Modules:
  0.0 939.8 jit_solution(3883574051171454138)
XLA Ops:
  7.9 19.7 %fusion.2 = f32[640,1024]{1,0:T(8,128)S(1)} fusion(f32[1,1,1024,1024]{3,2,1,0:T(8,128)} %param.7, f32[1024,128]{1,0:T(8,128)} %bitcast.56, f32[1024,512]{1,0:T(8,128)} %bitcast.55), kind=kOutput, calls=%fused_computation.33 | convolution fusion | flops 8053719040 | bytes 9437184 | tf_op jit(solution)/shard_map/dot_general | solution.py:36
  65.0 27.5 %reduce-scatter.25.cloned.1.call-done = f32[128,1]{1,0:T(8,128)} async-done(((f32[1024,1]{1,0:T(8,128)}), f32[128,1]{1,0:T(8,128)}) %reduce-scatter.25.cloned.1.call-update) | async-done | bytes 528
  93.4 34.3 %reduce-scatter.11.cloned.1.call-done = f32[128,128]{1,0:T(8,128)} async-done(((f32[1024,128]{1,0:T(8,128)}), f32[128,128]{1,0:T(8,128)}) %reduce-scatter.11.cloned.1.call-update) | async-done | bytes 65552 | tf_op jit(solution)/shard_map/reduce_scatter | solution.py:60
  128.7 17.3 %all_gather.21 = f32[1024,128]{1,0:T(8,128)} all-gather(f32[128,128]{1,0:T(8,128)S(1)} %broadcast_divide_fusion.1), channel_id=1, replica_groups=mesh['blk'=8,'sep'=32] {'blk'}, dimensions={0}, use_global_device_ids=true | all-gather | bytes 589824 | tf_op jit(solution)/shard_map/all_gather | solution.py:42
  153.6 9.0 collective-permute-done.2
  170.0 17.1 %collective-permute-done.3 = f32[1024,128]{1,0:T(8,128)} collective-permute-done((f32[1024,128]{1,0:T(8,128)}, f32[1024,128]{1,0:T(8,128)}, u32[]{:S(2)}, u32[]{:S(2)}) %collective-permute-start.3) | collective-permute-done | bytes 524320 | tf_op jit(solution)/shard_map/ppermute | solution.py:14
  191.4 25.9 %reduce-scatter.13.cloned.1.call-done = f32[128,128]{1,0:T(8,128)} async-done(((f32[1024,128]{1,0:T(8,128)}), f32[128,128]{1,0:T(8,128)}) %reduce-scatter.13.cloned.1.call-update) | async-done | bytes 65552 | tf_op jit(solution)/shard_map/reduce_scatter | solution.py:53
  218.3 16.9 %all_gather.22 = f32[1024,128]{1,0:T(8,128)} all-gather(f32[128,128]{1,0:T(8,128)S(1)} %divide_subtract_fusion.1), channel_id=1, replica_groups=mesh['blk'=8,'sep'=32] {'blk'}, dimensions={0}, use_global_device_ids=true | all-gather | bytes 589824 | tf_op jit(solution)/shard_map/all_gather | solution.py:42
  242.8 9.0 collective-permute-done.4
  259.5 17.1 %collective-permute-done.5 = f32[1024,128]{1,0:T(8,128)} collective-permute-done((f32[1024,128]{1,0:T(8,128)}, f32[1024,128]{1,0:T(8,128)}, u32[]{:S(2)}, u32[]{:S(2)}) %collective-permute-start.5) | collective-permute-done | bytes 524320 | tf_op jit(solution)/shard_map/ppermute | solution.py:14
  280.2 26.6 %reduce-scatter.15.cloned.1.call-done = f32[128,128]{1,0:T(8,128)} async-done(((f32[1024,128]{1,0:T(8,128)}), f32[128,128]{1,0:T(8,128)}) %reduce-scatter.15.cloned.1.call-update) | async-done | bytes 65552 | tf_op jit(solution)/shard_map/reduce_scatter | solution.py:53
  307.8 16.9 %all_gather.23 = f32[1024,128]{1,0:T(8,128)} all-gather(f32[128,128]{1,0:T(8,128)S(1)} %subtract_add_fusion.1), channel_id=1, replica_groups=mesh['blk'=8,'sep'=32] {'blk'}, dimensions={0}, use_global_device_ids=true | all-gather | bytes 589824 | tf_op jit(solution)/shard_map/all_gather | solution.py:42
  332.3 9.0 collective-permute-done.6
  348.8 17.1 %collective-permute-done.7 = f32[1024,128]{1,0:T(8,128)} collective-permute-done((f32[1024,128]{1,0:T(8,128)}, f32[1024,128]{1,0:T(8,128)}, u32[]{:S(2)}, u32[]{:S(2)}) %collective-permute-start.7) | collective-permute-done | bytes 524320 | tf_op jit(solution)/shard_map/ppermute | solution.py:14
  369.6 26.6 %reduce-scatter.17.cloned.1.call-done = f32[128,128]{1,0:T(8,128)} async-done(((f32[1024,128]{1,0:T(8,128)}), f32[128,128]{1,0:T(8,128)}) %reduce-scatter.17.cloned.1.call-update) | async-done | bytes 65552 | tf_op jit(solution)/shard_map/reduce_scatter | solution.py:53
  397.1 78.2 %all-reduce = (f32[128]{0:T(128)S(1)}, f32[128]{0:T(128)S(1)}) all-reduce(f32[128]{0:T(128)S(1)} %get-tuple-element.9, f32[128]{0:T(128)S(1)} %get-tuple-element.8), channel_id=1, replica_groups=mesh['blk'=8,'sep'=32] {'blk','sep'}, use_global_device_ids=true, to_apply=%region_13.14 | all-reduce | flops 256 | bytes 2048 | tf_op jit(solution)/shard_map/psum | solution.py:68
  476.8 14.9 %all_gather.24 = f32[1024,128]{1,0:T(8,128)} all-gather(f32[128,128]{1,0:T(8,128)S(1)} %broadcast_divide_fusion), channel_id=1, replica_groups=mesh['blk'=8,'sep'=32] {'blk'}, dimensions={0}, use_global_device_ids=true | all-gather | bytes 589824 | tf_op jit(solution)/shard_map/all_gather | solution.py:42
  495.6 10.1 %collective-permute-done.8 = f32[1024,128]{1,0:T(8,128)} collective-permute-done((f32[1024,128]{1,0:T(8,128)}, f32[1024,128]{1,0:T(8,128)}, u32[]{:S(2)}, u32[]{:S(2)}) %collective-permute-start.8) | collective-permute-done | bytes 524320 | tf_op jit(solution)/shard_map/ppermute | solution.py:14
  515.0 15.9 %collective-permute-done.9 = f32[1024,128]{1,0:T(8,128)} collective-permute-done((f32[1024,128]{1,0:T(8,128)}, f32[1024,128]{1,0:T(8,128)}, u32[]{:S(2)}, u32[]{:S(2)}) %collective-permute-start.9) | collective-permute-done | bytes 524320 | tf_op jit(solution)/shard_map/ppermute | solution.py:14
  534.9 26.6 %reduce-scatter.19.cloned.1.call-done = f32[128,128]{1,0:T(8,128)} async-done(((f32[1024,128]{1,0:T(8,128)}), f32[128,128]{1,0:T(8,128)}) %reduce-scatter.19.cloned.1.call-update) | async-done | bytes 65552 | tf_op jit(solution)/shard_map/reduce_scatter | solution.py:53
  562.4 16.9 %all_gather.25 = f32[1024,128]{1,0:T(8,128)} all-gather(f32[128,128]{1,0:T(8,128)S(1)} %divide_subtract_fusion), channel_id=1, replica_groups=mesh['blk'=8,'sep'=32] {'blk'}, dimensions={0}, use_global_device_ids=true | all-gather | bytes 589824 | tf_op jit(solution)/shard_map/all_gather | solution.py:42
  586.3 9.6 %collective-permute-done.10 = f32[1024,128]{1,0:T(8,128)} collective-permute-done((f32[1024,128]{1,0:T(8,128)}, f32[1024,128]{1,0:T(8,128)}, u32[]{:S(2)}, u32[]{:S(2)}) %collective-permute-start.10) | collective-permute-done | bytes 524320 | tf_op jit(solution)/shard_map/ppermute | solution.py:14
  604.3 17.1 %collective-permute-done.11 = f32[1024,128]{1,0:T(8,128)} collective-permute-done((f32[1024,128]{1,0:T(8,128)}, f32[1024,128]{1,0:T(8,128)}, u32[]{:S(2)}, u32[]{:S(2)}) %collective-permute-start.11) | collective-permute-done | bytes 524320 | tf_op jit(solution)/shard_map/ppermute | solution.py:14
  625.4 26.5 %reduce-scatter.21.cloned.1.call-done = f32[128,128]{1,0:T(8,128)} async-done(((f32[1024,128]{1,0:T(8,128)}), f32[128,128]{1,0:T(8,128)}) %reduce-scatter.21.cloned.1.call-update) | async-done | bytes 65552 | tf_op jit(solution)/shard_map/reduce_scatter | solution.py:53
  652.9 78.3 %psum.30 = f32[128]{0:T(128)S(1)} all-reduce(f32[128]{0:T(128)S(1)} %get-tuple-element.12), channel_id=1, replica_groups=mesh['blk'=8,'sep'=32] {'blk','sep'}, use_global_device_ids=true, to_apply=%region_26.27 | all-reduce | flops 128 | bytes 1024 | tf_op jit(solution)/shard_map/psum | solution.py:68
  731.8 15.2 %all_gather.26 = f32[1024,128]{1,0:T(8,128)} all-gather(f32[128,128]{1,0:T(8,128)S(1)} %multiply_add_fusion.1), channel_id=1, replica_groups=mesh['blk'=8,'sep'=32] {'blk'}, dimensions={0}, use_global_device_ids=true | all-gather | bytes 589824 | tf_op jit(solution)/shard_map/all_gather | solution.py:42
  751.3 9.4 collective-permute-done.12
  768.5 15.5 %collective-permute-done.13 = f32[1024,128]{1,0:T(8,128)S(1)} collective-permute-done((f32[1024,128]{1,0:T(8,128)S(1)}, f32[1024,128]{1,0:T(8,128)S(1)}, u32[]{:S(2)}, u32[]{:S(2)}) %collective-permute-start.13) | collective-permute-done | bytes 524320 | tf_op jit(solution)/shard_map/ppermute | solution.py:14
  787.0 26.6 %reduce-scatter.23.cloned.1.call-done = f32[128,128]{1,0:T(8,128)} async-done(((f32[1024,128]{1,0:T(8,128)}), f32[128,128]{1,0:T(8,128)}) %reduce-scatter.23.cloned.1.call-update) | async-done | bytes 65552 | tf_op jit(solution)/shard_map/reduce_scatter | solution.py:53
  814.5 78.2 %psum.31 = f32[128]{0:T(128)S(1)} all-reduce(f32[128]{0:T(128)S(1)} %multiply_reduce_fusion), channel_id=1, replica_groups=mesh['blk'=8,'sep'=32] {'blk','sep'}, use_global_device_ids=true, to_apply=%region_31.32 | all-reduce | flops 128 | bytes 1024 | tf_op jit(solution)/shard_map/psum | solution.py:68
  893.4 13.9 %all_gather.27 = f32[1024,128]{1,0:T(8,128)S(1)} all-gather(f32[128,128]{1,0:T(8,128)S(1)} %multiply_add_fusion), channel_id=1, replica_groups=mesh['blk'=8,'sep'=32] {'blk'}, dimensions={0}, use_global_device_ids=true | all-gather | bytes 589824 | tf_op jit(solution)/shard_map/all_gather | solution.py:42
  912.1 8.7 collective-permute-done.14
  (131 shorter events, 172.5 us)
Async XLA Ops:
  7.2 85.4 %reduce-scatter.25.cloned.1.call-start = ((), (), s32[]{:S(2)}) async-start(), calls=%async_computation.15 | async-start | bytes 589824
  7.9 159.8 %copy-start.11 = (s32[256,1]{0,1:T(1,128)}, s32[256,1]{0,1:T(1,128)S(1)}, u32[]{:S(2)}) copy-start(s32[256,1]{0,1:T(1,128)S(1)} %get-tuple-element.19) | copy-start | bytes 3076
  36.5 24.8 %collective-permute-start = (f32[1024,128]{1,0:T(8,128)}, f32[1024,128]{1,0:T(8,128)}, u32[]{:S(2)}, u32[]{:S(2)}) collective-permute-start(f32[1024,128]{1,0:T(8,128)} %scatter_custom_fusion), channel_id=1, source_target_pairs={{0,1},{1,2},{2,3},{3,4},{4,5},{5,6},{6,7},{7,8},{8,9},{9,10},{10,1... | collective-permute-start | bytes 1572872 | tf_op jit(solution)/shard_map/ppermute | solution.py:14
  50.1 7.7 collective-permute-start.1
  61.1 66.6 %reduce-scatter.11.cloned.1.call-start = ((), (), s32[]{:S(2)}) async-start(), calls=%async_computation.8 | async-start | bytes 589824 | tf_op jit(solution)/shard_map/reduce_scatter | solution.py:60
  64.9 152.4 %reduce-scatter.13.cloned.1.call-start = ((), (), s32[]{:S(2)}) async-start(), calls=%async_computation.9 | async-start | bytes 589824 | tf_op jit(solution)/shard_map/reduce_scatter | solution.py:53
  146.0 16.6 %collective-permute-start.2 = (f32[1024,128]{1,0:T(8,128)}, f32[1024,128]{1,0:T(8,128)}, u32[]{:S(2)}, u32[]{:S(2)}) collective-permute-start(f32[1024,128]{1,0:T(8,128)} %all_gather.21), channel_id=1, source_target_pairs={{0,31},{1,0},{2,1},{3,2},{4,3},{5,4},{6,5},{7,6},{8,7},{9,8},{10,9... | collective-permute-start | bytes 1572872 | tf_op jit(solution)/shard_map/ppermute | solution.py:14
  151.2 66.2 %copy-start.1 = (f32[128,128]{1,0:T(8,128)S(1)}, f32[128,128]{1,0:T(8,128)}, u32[]{:S(2)}) copy-start(f32[128,128]{1,0:T(8,128)} %reduce-scatter.11.cloned.1.call-done) | copy-start | bytes 196612
  170.0 17.1 %collective-permute-start.3 = (f32[1024,128]{1,0:T(8,128)}, f32[1024,128]{1,0:T(8,128)}, u32[]{:S(2)}, u32[]{:S(2)}) collective-permute-start(f32[1024,128]{1,0:T(8,128)} %scatter_custom_fusion.4), channel_id=1, source_target_pairs={{0,1},{1,2},{2,3},{3,4},{4,5},{5,6},{6,7},{7,8},{8,9},{9,10},{10,1... | collective-permute-start | bytes 1572872 | tf_op jit(solution)/shard_map/ppermute | solution.py:14
  190.7 116.1 %reduce-scatter.15.cloned.1.call-start = ((), (), s32[]{:S(2)}) async-start(), calls=%async_computation.10 | async-start | bytes 589824 | tf_op jit(solution)/shard_map/reduce_scatter | solution.py:53
  191.4 60.4 %copy-start.7 = (f32[128]{0:T(128)}, f32[128]{0:T(128)S(1)}, u32[]{:S(2)}) copy-start(f32[128]{0:T(128)S(1)} %multiply_bitcast_fusion) | copy-start | bytes 1540
  235.2 71.6 %copy-start.6 = (f32[128,128]{1,0:T(8,128)S(1)}, f32[128,128]{1,0:T(8,128)}, u32[]{:S(2)}) copy-start(f32[128,128]{1,0:T(8,128)} %reduce-scatter.13.cloned.1.call-done) | copy-start | bytes 196612
  235.2 16.6 %collective-permute-start.4 = (f32[1024,128]{1,0:T(8,128)}, f32[1024,128]{1,0:T(8,128)}, u32[]{:S(2)}, u32[]{:S(2)}) collective-permute-start(f32[1024,128]{1,0:T(8,128)} %all_gather.22), channel_id=1, source_target_pairs={{0,31},{1,0},{2,1},{3,2},{4,3},{5,4},{6,5},{7,6},{8,7},{9,8},{10,9... | collective-permute-start | bytes 1572872 | tf_op jit(solution)/shard_map/ppermute | solution.py:14
  259.3 17.3 %collective-permute-start.5 = (f32[1024,128]{1,0:T(8,128)}, f32[1024,128]{1,0:T(8,128)}, u32[]{:S(2)}, u32[]{:S(2)}) collective-permute-start(f32[1024,128]{1,0:T(8,128)} %scatter_custom_fusion.6), channel_id=1, source_target_pairs={{0,1},{1,2},{2,3},{3,4},{4,5},{5,6},{6,7},{7,8},{8,9},{9,10},{10,1... | collective-permute-start | bytes 1572872 | tf_op jit(solution)/shard_map/ppermute | solution.py:14
  280.2 116.0 %reduce-scatter.17.cloned.1.call-start = ((), (), s32[]{:S(2)}) async-start(), calls=%async_computation.11 | async-start | bytes 589824 | tf_op jit(solution)/shard_map/reduce_scatter | solution.py:53
  324.7 16.6 %collective-permute-start.6 = (f32[1024,128]{1,0:T(8,128)}, f32[1024,128]{1,0:T(8,128)}, u32[]{:S(2)}, u32[]{:S(2)}) collective-permute-start(f32[1024,128]{1,0:T(8,128)} %all_gather.23), channel_id=1, source_target_pairs={{0,31},{1,0},{2,1},{3,2},{4,3},{5,4},{6,5},{7,6},{8,7},{9,8},{10,9... | collective-permute-start | bytes 1572872 | tf_op jit(solution)/shard_map/ppermute | solution.py:14
  348.8 17.1 %collective-permute-start.7 = (f32[1024,128]{1,0:T(8,128)}, f32[1024,128]{1,0:T(8,128)}, u32[]{:S(2)}, u32[]{:S(2)}) collective-permute-start(f32[1024,128]{1,0:T(8,128)} %scatter_custom_fusion.8), channel_id=1, source_target_pairs={{0,1},{1,2},{2,3},{3,4},{4,5},{5,6},{6,7},{7,8},{8,9},{9,10},{10,1... | collective-permute-start | bytes 1572872 | tf_op jit(solution)/shard_map/ppermute | solution.py:14
  369.6 191.9 %reduce-scatter.19.cloned.1.call-start = ((), (), s32[]{:S(2)}) async-start(), calls=%async_computation.12 | async-start | bytes 589824 | tf_op jit(solution)/shard_map/reduce_scatter | solution.py:53
  491.7 69.8 %copy-start.8 = (f32[128]{0:T(128)S(1)}, f32[128]{0:T(128)}, u32[]{:S(2)}) copy-start(f32[128]{0:T(128)} %copy-done.7) | copy-start | bytes 1540
  491.7 14.0 %collective-permute-start.8 = (f32[1024,128]{1,0:T(8,128)}, f32[1024,128]{1,0:T(8,128)}, u32[]{:S(2)}, u32[]{:S(2)}) collective-permute-start(f32[1024,128]{1,0:T(8,128)} %all_gather.24), channel_id=1, source_target_pairs={{0,31},{1,0},{2,1},{3,2},{4,3},{5,4},{6,5},{7,6},{8,7},{9,8},{10,9... | collective-permute-start | bytes 1572872 | tf_op jit(solution)/shard_map/ppermute | solution.py:14
  514.0 16.8 %collective-permute-start.9 = (f32[1024,128]{1,0:T(8,128)}, f32[1024,128]{1,0:T(8,128)}, u32[]{:S(2)}, u32[]{:S(2)}) collective-permute-start(f32[1024,128]{1,0:T(8,128)} %scatter_custom_fusion.10), channel_id=1, source_target_pairs={{0,1},{1,2},{2,3},{3,4},{4,5},{5,6},{6,7},{7,8},{8,9},{9,10},{10,1... | collective-permute-start | bytes 1572872 | tf_op jit(solution)/shard_map/ppermute | solution.py:14
  534.8 117.1 %reduce-scatter.21.cloned.1.call-start = ((), (), s32[]{:S(2)}) async-start(), calls=%async_computation.13 | async-start | bytes 589824 | tf_op jit(solution)/shard_map/reduce_scatter | solution.py:53
  579.3 72.6 %copy-start.2 = (f32[128,128]{1,0:T(8,128)S(1)}, f32[128,128]{1,0:T(8,128)}, u32[]{:S(2)}) copy-start(f32[128,128]{1,0:T(8,128)} %reduce-scatter.17.cloned.1.call-done) | copy-start | bytes 196612
  579.3 16.6 %collective-permute-start.10 = (f32[1024,128]{1,0:T(8,128)}, f32[1024,128]{1,0:T(8,128)}, u32[]{:S(2)}, u32[]{:S(2)}) collective-permute-start(f32[1024,128]{1,0:T(8,128)} %all_gather.25), channel_id=1, source_target_pairs={{0,31},{1,0},{2,1},{3,2},{4,3},{5,4},{6,5},{7,6},{8,7},{9,8},{10,9... | collective-permute-start | bytes 1572872 | tf_op jit(solution)/shard_map/ppermute | solution.py:14
  604.3 17.1 %collective-permute-start.11 = (f32[1024,128]{1,0:T(8,128)}, f32[1024,128]{1,0:T(8,128)}, u32[]{:S(2)}, u32[]{:S(2)}) collective-permute-start(f32[1024,128]{1,0:T(8,128)} %scatter_custom_fusion.12), channel_id=1, source_target_pairs={{0,1},{1,2},{2,3},{3,4},{4,5},{5,6},{6,7},{7,8},{8,9},{9,10},{10,1... | collective-permute-start | bytes 1572872 | tf_op jit(solution)/shard_map/ppermute | solution.py:14
  625.4 188.2 %reduce-scatter.23.cloned.1.call-start = ((), (), s32[]{:S(2)}) async-start(), calls=%async_computation.14 | async-start | bytes 589824 | tf_op jit(solution)/shard_map/reduce_scatter | solution.py:53
  731.2 29.5 %copy-start.13 = (f32[128]{0:T(128)}, f32[128]{0:T(128)S(1)}, u32[]{:S(2)}) copy-start(f32[128]{0:T(128)S(1)} %psum.30) | copy-start | bytes 1540
  747.0 13.6 %collective-permute-start.12 = (f32[1024,128]{1,0:T(8,128)}, f32[1024,128]{1,0:T(8,128)}, u32[]{:S(2)}, u32[]{:S(2)}) collective-permute-start(f32[1024,128]{1,0:T(8,128)} %all_gather.26), channel_id=1, source_target_pairs={{0,31},{1,0},{2,1},{3,2},{4,3},{5,4},{6,5},{7,6},{8,7},{9,8},{10,9... | collective-permute-start | bytes 1572872 | tf_op jit(solution)/shard_map/ppermute | solution.py:14
  751.3 142.1 %copy-start.10 = (f32[128]{0:T(128)S(1)}, f32[128]{0:T(128)}, u32[]{:S(2)}) copy-start(f32[128]{0:T(128)} %copy-done.9) | copy-start | bytes 1540
  767.5 16.5 %collective-permute-start.13 = (f32[1024,128]{1,0:T(8,128)S(1)}, f32[1024,128]{1,0:T(8,128)S(1)}, u32[]{:S(2)}, u32[]{:S(2)}) collective-permute-start(f32[1024,128]{1,0:T(8,128)S(1)} %scatter_custom_fusion.14), channel_id=1, source_target_pairs={{0,1},{1,2},{2,3},{3,4},{4,5},{5,6},{6,7},{7,8},{8,9},{9,10},{10,1... | collective-permute-start | bytes 1572872 | tf_op jit(solution)/shard_map/ppermute | solution.py:14
  893.4 31.6 %copy-start.4 = (f32[128,128]{1,0:T(8,128)}, f32[128,128]{1,0:T(8,128)S(1)}, u32[]{:S(2)}) copy-start(f32[128,128]{1,0:T(8,128)S(1)} %multiply_add_fusion) | copy-start | bytes 196612
  907.2 13.6 %collective-permute-start.14 = (f32[1024,128]{1,0:T(8,128)S(1)}, f32[1024,128]{1,0:T(8,128)S(1)}, u32[]{:S(2)}, u32[]{:S(2)}) collective-permute-start(f32[1024,128]{1,0:T(8,128)S(1)} %all_gather.27), channel_id=1, source_target_pairs={{0,31},{1,0},{2,1},{3,2},{4,3},{5,4},{6,5},{7,6},{8,7},{9,8},{10,9... | collective-permute-start | bytes 1572872 | tf_op jit(solution)/shard_map/ppermute | solution.py:14
  (5 other events, 42.3 us)
Sparse Core Ops, SparseCore 0:
  61.3 31.2 reduce-scatter.24
  95.0 32.6 reduce-scatter.10
  190.8 26.4 reduce-scatter.12
  280.3 26.4 reduce-scatter.14
  369.7 26.4 reduce-scatter.16
  535.0 26.4 reduce-scatter.18
  625.5 26.3 reduce-scatter.20
  787.1 26.4 reduce-scatter.22
where the time goes:
time: 948 us; the launch traced here: 940 us
  waiting for transfers between devices  391 us (41%)
  blocking collectives  347 us (37%)
  other arithmetic  57.1 us (6%)
  matrix products  52.9 us (6%)
  local copies, waits for them, and re-layouts  42.7 us (5%)
  starting transfers between devices  33.4 us (4%)
  between operations  15.6 us (2%)
    psum x3, blocking collectives, column_sum(): return lax.psum(jnp.sum(left * right, axis=0), ('blk', 'sep'))  235 us
    ppermute x15, waiting for transfers between devices, shifted(): lax.ppermute(array, axis, [(i, (i + by) % devices) for i in range(devices)])  171 us
    reduce_scatter x6, waiting for transfers between devices, collect(): lax.psum_scatter(own_part + back, 'blk', scatter_dimension=0, tiled=True)  159 us
    all_gather x7, blocking collectives, spread(): whole = lax.all_gather(owned, 'blk', axis=0, tiled=True)  112 us
    reduce_scatter x1, waiting for transfers between devices, body(): lax.psum_scatter(own_main + back_main, 'blk', scatter_dimension=0, tiled=...  34.3 us
    ppermute x15, starting transfers between devices, shifted(): lax.ppermute(array, axis, [(i, (i + by) % devices) for i in range(devices)])  33 us
    gather x14, local copies, waits for them, and re-layouts, spread(): return jnp.concatenate([whole[lower], after[higher]], axis=0)  29 us
    unnamed x9, waiting for transfers between devices  27.7 us
  transfers between devices with their start and end apart: 23, of which 22 were waited for; matrix products, arithmetic and copies ran while one was open for 4% of the time, Pallas kernels for 0%

commit v1 on v0

--- a/solution.py
+++ b/solution.py
@@ -2,6 +2,7 @@
 import jax.numpy as jnp
 from jax import lax
 from jax.sharding import PartitionSpec as P
+from jax.lax import all_to_all, axis_size
 
 SEP_PORTS = 1024
 ITERS = 2
@@ -39,7 +40,8 @@
     reduced = outer - reduced_all[:, width:]
 
     def spread(owned):
-        whole = lax.all_gather(owned, "blk", axis=0, tiled=True)
+        carry = jnp.concatenate([owned for _ in range(axis_size("blk"))], 0)
+        whole = all_to_all(carry, "blk", 0, 0, tiled=True)
         after = shifted(whole, "sep", -1)
         return jnp.concatenate([whole[lower], after[higher]], axis=0)
 

time: 948 us -> 938 us (0.989)
  blocking collectives: 347 us -> 335 us
    all_gather x7 -> x0, blocking collectives: 112 us -> none  [spread(): whole = lax.all_gather(owned, 'blk', axis=0, tiled=True)]
    all_to_all x0 -> x7, blocking collectives: none -> 101 us  [spread(): whole = all_to_all(carry, 'blk', 0, 0, tiled=True)]
    ppermute x15, waiting for transfers between devices: 171 us -> 159 us  [shifted(): lax.ppermute(array, axis, [(i, (i + by) % devices) for i in range(devices)])]
    unnamed x0 -> x13, other arithmetic: none -> 10.3 us
where the time goes in v1:
time: 938 us; the launch traced here: 930 us
  waiting for transfers between devices  383 us (41%)
  blocking collectives  335 us (36%)
  other arithmetic  65 us (7%)
  matrix products  53.6 us (6%)
  local copies, waits for them, and re-layouts  43 us (5%)
  starting transfers between devices  33.5 us (4%)
  between operations  15.9 us (2%)
    psum x3, blocking collectives, column_sum(): return lax.psum(jnp.sum(left * right, axis=0), ('blk', 'sep'))  235 us
    reduce_scatter x6, waiting for transfers between devices, collect(): lax.psum_scatter(own_part + back, 'blk', scatter_dimension=0, tiled=True)  162 us
    ppermute x15, waiting for transfers between devices, shifted(): lax.ppermute(array, axis, [(i, (i + by) % devices) for i in range(devices)])  159 us
    all_to_all x7, blocking collectives, spread(): whole = all_to_all(carry, 'blk', 0, 0, tiled=True)  101 us
    reduce_scatter x1, waiting for transfers between devices, body(): lax.psum_scatter(own_main + back_main, 'blk', scatter_dimension=0, tiled=...  34.3 us
    ppermute x15, starting transfers between devices, shifted(): lax.ppermute(array, axis, [(i, (i + by) % devices) for i in range(devices)])  33.2 us
    gather x14, local copies, waits for them, and re-layouts, spread(): return jnp.concatenate([whole[lower], after[higher]], axis=0)  29 us
    unnamed x9, waiting for transfers between devices  27.7 us
  transfers between devices with their start and end apart: 23, of which 22 were waited for; matrix products, arithmetic and copies ran while one was open for 4% of the time, Pallas kernels for 0%

profile of v1, /device:TPU:1, one launch (start us, length us, event | category | flops | bytes accessed | tf_op | source)
XLA Modules:
  0.0 929.7 jit_solution(4796296511614965544)
XLA Ops:
  7.9 19.7 %fusion.2 = f32[640,1024]{1,0:T(8,128)S(1)} fusion(f32[1,1,1024,1024]{3,2,1,0:T(8,128)} %param.7, f32[1024,128]{1,0:T(8,128)} %bitcast.80, f32[1024,512]{1,0:T(8,128)} %bitcast.69), kind=kOutput, calls=%fused_computation.33 | convolution fusion | flops 8053719040 | bytes 9437184 | tf_op jit(solution)/shard_map/dot_general | solution.py:37
  65.0 27.5 %reduce-scatter.25.cloned.1.call-done = f32[128,1]{1,0:T(8,128)} async-done(((f32[1024,1]{1,0:T(8,128)}), f32[128,1]{1,0:T(8,128)}) %reduce-scatter.25.cloned.1.call-update) | async-done | bytes 528
  93.4 34.3 %reduce-scatter.11.cloned.1.call-done = f32[128,128]{1,0:T(8,128)} async-done(((f32[1024,128]{1,0:T(8,128)}), f32[128,128]{1,0:T(8,128)}) %reduce-scatter.11.cloned.1.call-update) | async-done | bytes 65552 | tf_op jit(solution)/shard_map/reduce_scatter | solution.py:62
  135.2 15.3 %all_to_all.84 = f32[8,128,128]{2,1,0:T(8,128)} all-to-all(f32[8,128,128]{2,1,0:T(8,128)S(1)} %bitcast.74), channel_id=1, replica_groups=mesh['blk'=8,'sep'=32] {'blk'}, dimensions={0} | all-to-all | bytes 1048576 | tf_op jit(solution)/shard_map/all_to_all | solution.py:44
  158.6 8.1 collective-permute-done.2
  174.1 16.2 %collective-permute-done.3 = f32[1024,128]{1,0:T(8,128)} collective-permute-done((f32[1024,128]{1,0:T(8,128)}, f32[1024,128]{1,0:T(8,128)}, u32[]{:S(2)}, u32[]{:S(2)}) %collective-permute-start.3) | collective-permute-done | bytes 524320 | tf_op jit(solution)/shard_map/ppermute | solution.py:15
  194.7 26.5 %reduce-scatter.13.cloned.1.call-done = f32[128,128]{1,0:T(8,128)} async-done(((f32[1024,128]{1,0:T(8,128)}), f32[128,128]{1,0:T(8,128)}) %reduce-scatter.13.cloned.1.call-update) | async-done | bytes 65552 | tf_op jit(solution)/shard_map/reduce_scatter | solution.py:55
  222.2 15.3 %all_to_all.85 = f32[8,128,128]{2,1,0:T(8,128)} all-to-all(f32[8,128,128]{2,1,0:T(8,128)S(1)} %bitcast.77), channel_id=1, replica_groups=mesh['blk'=8,'sep'=32] {'blk'}, dimensions={0} | all-to-all | bytes 1048576 | tf_op jit(solution)/shard_map/all_to_all | solution.py:44
  244.5 8.8 collective-permute-done.4
  261.6 16.2 %collective-permute-done.5 = f32[1024,128]{1,0:T(8,128)} collective-permute-done((f32[1024,128]{1,0:T(8,128)}, f32[1024,128]{1,0:T(8,128)}, u32[]{:S(2)}, u32[]{:S(2)}) %collective-permute-start.5) | collective-permute-done | bytes 524320 | tf_op jit(solution)/shard_map/ppermute | solution.py:15
  281.9 27.2 %reduce-scatter.15.cloned.1.call-done = f32[128,128]{1,0:T(8,128)} async-done(((f32[1024,128]{1,0:T(8,128)}), f32[128,128]{1,0:T(8,128)}) %reduce-scatter.15.cloned.1.call-update) | async-done | bytes 65552 | tf_op jit(solution)/shard_map/reduce_scatter | solution.py:55
  310.2 15.3 %all_to_all.86 = f32[8,128,128]{2,1,0:T(8,128)} all-to-all(f32[8,128,128]{2,1,0:T(8,128)S(1)} %bitcast.73), channel_id=1, replica_groups=mesh['blk'=8,'sep'=32] {'blk'}, dimensions={0} | all-to-all | bytes 1048576 | tf_op jit(solution)/shard_map/all_to_all | solution.py:44
  333.2 8.1 collective-permute-done.6
  348.8 16.2 %collective-permute-done.7 = f32[1024,128]{1,0:T(8,128)} collective-permute-done((f32[1024,128]{1,0:T(8,128)}, f32[1024,128]{1,0:T(8,128)}, u32[]{:S(2)}, u32[]{:S(2)}) %collective-permute-start.7) | collective-permute-done | bytes 524320 | tf_op jit(solution)/shard_map/ppermute | solution.py:15
  368.7 27.1 %reduce-scatter.17.cloned.1.call-done = f32[128,128]{1,0:T(8,128)} async-done(((f32[1024,128]{1,0:T(8,128)}), f32[128,128]{1,0:T(8,128)}) %reduce-scatter.17.cloned.1.call-update) | async-done | bytes 65552 | tf_op jit(solution)/shard_map/reduce_scatter | solution.py:55
  396.8 78.2 %all-reduce = (f32[128]{0:T(128)S(1)}, f32[128]{0:T(128)S(1)}) all-reduce(f32[128]{0:T(128)S(1)} %get-tuple-element.9, f32[128]{0:T(128)S(1)} %get-tuple-element.8), channel_id=1, replica_groups=mesh['blk'=8,'sep'=32] {'blk','sep'}, use_global_device_ids=true, to_apply=%region_13.14 | all-reduce | flops 256 | bytes 2048 | tf_op jit(solution)/shard_map/psum | solution.py:70
  476.6 13.3 %all_to_all.87 = f32[8,128,128]{2,1,0:T(8,128)} all-to-all(f32[8,128,128]{2,1,0:T(8,128)S(1)} %bitcast.78), channel_id=1, replica_groups=mesh['blk'=8,'sep'=32] {'blk'}, dimensions={0} | all-to-all | bytes 1048576 | tf_op jit(solution)/shard_map/all_to_all | solution.py:44
  493.5 9.2 collective-permute-done.8
  512.0 14.9 %collective-permute-done.9 = f32[1024,128]{1,0:T(8,128)} collective-permute-done((f32[1024,128]{1,0:T(8,128)}, f32[1024,128]{1,0:T(8,128)}, u32[]{:S(2)}, u32[]{:S(2)}) %collective-permute-start.9) | collective-permute-done | bytes 524320 | tf_op jit(solution)/shard_map/ppermute | solution.py:15
  530.9 27.2 %reduce-scatter.19.cloned.1.call-done = f32[128,128]{1,0:T(8,128)} async-done(((f32[1024,128]{1,0:T(8,128)}), f32[128,128]{1,0:T(8,128)}) %reduce-scatter.19.cloned.1.call-update) | async-done | bytes 65552 | tf_op jit(solution)/shard_map/reduce_scatter | solution.py:55
  559.1 15.3 %all_to_all.88 = f32[8,128,128]{2,1,0:T(8,128)} all-to-all(f32[8,128,128]{2,1,0:T(8,128)S(1)} %bitcast.79), channel_id=1, replica_groups=mesh['blk'=8,'sep'=32] {'blk'}, dimensions={0} | all-to-all | bytes 1048576 | tf_op jit(solution)/shard_map/all_to_all | solution.py:44
  582.2 8.1 collective-permute-done.10
  598.8 16.2 %collective-permute-done.11 = f32[1024,128]{1,0:T(8,128)} collective-permute-done((f32[1024,128]{1,0:T(8,128)}, f32[1024,128]{1,0:T(8,128)}, u32[]{:S(2)}, u32[]{:S(2)}) %collective-permute-start.11) | collective-permute-done | bytes 524320 | tf_op jit(solution)/shard_map/ppermute | solution.py:15
  619.1 27.2 %reduce-scatter.21.cloned.1.call-done = f32[128,128]{1,0:T(8,128)} async-done(((f32[1024,128]{1,0:T(8,128)}), f32[128,128]{1,0:T(8,128)}) %reduce-scatter.21.cloned.1.call-update) | async-done | bytes 65552 | tf_op jit(solution)/shard_map/reduce_scatter | solution.py:55
  647.7 78.3 %psum.30 = f32[128]{0:T(128)S(1)} all-reduce(f32[128]{0:T(128)} %get-tuple-element.16), channel_id=1, replica_groups=mesh['blk'=8,'sep'=32] {'blk','sep'}, use_global_device_ids=true, to_apply=%region_26.27 | all-reduce | flops 128 | bytes 1024 | tf_op jit(solution)/shard_map/psum | solution.py:70
  726.7 13.3 %all_to_all.89 = f32[8,128,128]{2,1,0:T(8,128)} all-to-all(f32[8,128,128]{2,1,0:T(8,128)S(1)} %bitcast.76), channel_id=1, replica_groups=mesh['blk'=8,'sep'=32] {'blk'}, dimensions={0} | all-to-all | bytes 1048576 | tf_op jit(solution)/shard_map/all_to_all | solution.py:44
  744.3 8.5 collective-permute-done.12
  760.7 14.6 %collective-permute-done.13 = f32[1024,128]{1,0:T(8,128)S(1)} collective-permute-done((f32[1024,128]{1,0:T(8,128)S(1)}, f32[1024,128]{1,0:T(8,128)S(1)}, u32[]{:S(2)}, u32[]{:S(2)}) %collective-permute-start.13) | collective-permute-done | bytes 524320 | tf_op jit(solution)/shard_map/ppermute | solution.py:15
  778.5 27.2 %reduce-scatter.23.cloned.1.call-done = f32[128,128]{1,0:T(8,128)} async-done(((f32[1024,128]{1,0:T(8,128)}), f32[128,128]{1,0:T(8,128)}) %reduce-scatter.23.cloned.1.call-update) | async-done | bytes 65552 | tf_op jit(solution)/shard_map/reduce_scatter | solution.py:55
  806.6 78.2 %psum.31 = f32[128]{0:T(128)S(1)} all-reduce(f32[128]{0:T(128)S(1)} %multiply_reduce_fusion), channel_id=1, replica_groups=mesh['blk'=8,'sep'=32] {'blk','sep'}, use_global_device_ids=true, to_apply=%region_31.32 | all-reduce | flops 128 | bytes 1024 | tf_op jit(solution)/shard_map/psum | solution.py:70
  885.6 12.7 %all_to_all.90 = f32[8,128,128]{2,1,0:T(8,128)S(1)} all-to-all(f32[8,128,128]{2,1,0:T(8,128)S(1)} %bitcast.75), channel_id=1, replica_groups=mesh['blk'=8,'sep'=32] {'blk'}, dimensions={0} | all-to-all | bytes 1048576 | tf_op jit(solution)/shard_map/all_to_all | solution.py:44
  902.9 7.9 collective-permute-done.14
  (178 shorter events, 181.5 us)
Async XLA Ops:
  7.2 85.4 %reduce-scatter.25.cloned.1.call-start = ((), (), s32[]{:S(2)}) async-start(), calls=%async_computation.22 | async-start | bytes 589824
  7.9 251.2 %copy-start.10 = (s32[256,1]{0,1:T(1,128)}, s32[256,1]{0,1:T(1,128)S(1)}, u32[]{:S(2)}) copy-start(s32[256,1]{0,1:T(1,128)S(1)} %get-tuple-element.31) | copy-start | bytes 3076
  7.9 19.7 %copy-start.1 = (f32[1,1,1024,512]{3,2,1,0:T(8,128)S(1)}, f32[1,1,1024,512]{3,2,1,0:T(8,128)}, u32[]{:S(2)}) copy-start(f32[1,1,1024,512]{3,2,1,0:T(8,128)} %param.8) | copy-start | bytes 6291460
  36.5 24.8 %collective-permute-start = (f32[1024,128]{1,0:T(8,128)}, f32[1024,128]{1,0:T(8,128)}, u32[]{:S(2)}, u32[]{:S(2)}) collective-permute-start(f32[1024,128]{1,0:T(8,128)} %scatter_custom_fusion), channel_id=1, source_target_pairs={{0,1},{1,2},{2,3},{3,4},{4,5},{5,6},{6,7},{7,8},{8,9},{9,10},{10,1... | collective-permute-start | bytes 1572872 | tf_op jit(solution)/shard_map/ppermute | solution.py:15
  50.1 7.7 collective-permute-start.1
  61.2 66.6 %reduce-scatter.11.cloned.1.call-start = ((), (), s32[]{:S(2)}) async-start(), calls=%async_computation.15 | async-start | bytes 589824 | tf_op jit(solution)/shard_map/reduce_scatter | solution.py:62
  64.9 156.2 %reduce-scatter.13.cloned.1.call-start = ((), (), s32[]{:S(2)}) async-start(), calls=%async_computation.16 | async-start | bytes 589824 | tf_op jit(solution)/shard_map/reduce_scatter | solution.py:55
  150.5 16.2 %collective-permute-start.2 = (f32[1024,128]{1,0:T(8,128)}, f32[1024,128]{1,0:T(8,128)}, u32[]{:S(2)}, u32[]{:S(2)}) collective-permute-start(f32[1024,128]{1,0:T(8,128)} %bitcast.17), channel_id=1, source_target_pairs={{0,31},{1,0},{2,1},{3,2},{4,3},{5,4},{6,5},{7,6},{8,7},{9,8},{10,9... | collective-permute-start | bytes 1572872 | tf_op jit(solution)/shard_map/ppermute | solution.py:15
  156.2 65.0 %copy-start = (f32[128,128]{1,0:T(8,128)S(1)}, f32[128,128]{1,0:T(8,128)}, u32[]{:S(2)}) copy-start(f32[128,128]{1,0:T(8,128)} %reduce-scatter.11.cloned.1.call-done) | copy-start | bytes 196612
  174.1 16.2 %collective-permute-start.3 = (f32[1024,128]{1,0:T(8,128)}, f32[1024,128]{1,0:T(8,128)}, u32[]{:S(2)}, u32[]{:S(2)}) collective-permute-start(f32[1024,128]{1,0:T(8,128)} %scatter_custom_fusion.4), channel_id=1, source_target_pairs={{0,1},{1,2},{2,3},{3,4},{4,5},{5,6},{6,7},{7,8},{8,9},{9,10},{10,1... | collective-permute-start | bytes 1572872 | tf_op jit(solution)/shard_map/ppermute | solution.py:15
  194.0 115.1 %reduce-scatter.15.cloned.1.call-start = ((), (), s32[]{:S(2)}) async-start(), calls=%async_computation.17 | async-start | bytes 589824 | tf_op jit(solution)/shard_map/reduce_scatter | solution.py:55
  194.7 114.4 %copy-start.6 = (f32[128]{0:T(128)}, f32[128]{0:T(128)S(1)}, u32[]{:S(2)}) copy-start(f32[128]{0:T(128)S(1)} %multiply_bitcast_fusion) | copy-start | bytes 1540
  237.6 15.7 %collective-permute-start.4 = (f32[1024,128]{1,0:T(8,128)}, f32[1024,128]{1,0:T(8,128)}, u32[]{:S(2)}, u32[]{:S(2)}) collective-permute-start(f32[1024,128]{1,0:T(8,128)} %bitcast.20), channel_id=1, source_target_pairs={{0,31},{1,0},{2,1},{3,2},{4,3},{5,4},{6,5},{7,6},{8,7},{9,8},{10,9... | collective-permute-start | bytes 1572872 | tf_op jit(solution)/shard_map/ppermute | solution.py:15
  261.6 16.2 %collective-permute-start.5 = (f32[1024,128]{1,0:T(8,128)}, f32[1024,128]{1,0:T(8,128)}, u32[]{:S(2)}, u32[]{:S(2)}) collective-permute-start(f32[1024,128]{1,0:T(8,128)} %scatter_custom_fusion.6), channel_id=1, source_target_pairs={{0,1},{1,2},{2,3},{3,4},{4,5},{5,6},{6,7},{7,8},{8,9},{9,10},{10,1... | collective-permute-start | bytes 1572872 | tf_op jit(solution)/shard_map/ppermute | solution.py:15
  281.9 114.0 %reduce-scatter.17.cloned.1.call-start = ((), (), s32[]{:S(2)}) async-start(), calls=%async_computation.18 | async-start | bytes 589824 | tf_op jit(solution)/shard_map/reduce_scatter | solution.py:55
  325.5 15.9 %collective-permute-start.6 = (f32[1024,128]{1,0:T(8,128)}, f32[1024,128]{1,0:T(8,128)}, u32[]{:S(2)}, u32[]{:S(2)}) collective-permute-start(f32[1024,128]{1,0:T(8,128)} %bitcast.22), channel_id=1, source_target_pairs={{0,31},{1,0},{2,1},{3,2},{4,3},{5,4},{6,5},{7,6},{8,7},{9,8},{10,9... | collective-permute-start | bytes 1572872 | tf_op jit(solution)/shard_map/ppermute | solution.py:15
  348.8 16.2 %collective-permute-start.7 = (f32[1024,128]{1,0:T(8,128)}, f32[1024,128]{1,0:T(8,128)}, u32[]{:S(2)}, u32[]{:S(2)}) collective-permute-start(f32[1024,128]{1,0:T(8,128)} %scatter_custom_fusion.8), channel_id=1, source_target_pairs={{0,1},{1,2},{2,3},{3,4},{4,5},{5,6},{6,7},{7,8},{8,9},{9,10},{10,1... | collective-permute-start | bytes 1572872 | tf_op jit(solution)/shard_map/ppermute | solution.py:15
  368.7 189.4 %reduce-scatter.19.cloned.1.call-start = ((), (), s32[]{:S(2)}) async-start(), calls=%async_computation.19 | async-start | bytes 589824 | tf_op jit(solution)/shard_map/reduce_scatter | solution.py:55
  475.5 14.4 %copy-start.8 = (f32[128]{0:T(128)}, f32[128]{0:T(128)S(1)}, u32[]{:S(2)}) copy-start(f32[128]{0:T(128)S(1)} %div.60) | copy-start | bytes 1540
  489.9 68.2 %copy-start.7 = (f32[128]{0:T(128)S(1)}, f32[128]{0:T(128)}, u32[]{:S(2)}) copy-start(f32[128]{0:T(128)} %copy-done.6) | copy-start | bytes 1540
  489.9 12.8 %collective-permute-start.8 = (f32[1024,128]{1,0:T(8,128)}, f32[1024,128]{1,0:T(8,128)}, u32[]{:S(2)}, u32[]{:S(2)}) collective-permute-start(f32[1024,128]{1,0:T(8,128)} %bitcast.24), channel_id=1, source_target_pairs={{0,31},{1,0},{2,1},{3,2},{4,3},{5,4},{6,5},{7,6},{8,7},{9,8},{10,9... | collective-permute-start | bytes 1572872 | tf_op jit(solution)/shard_map/ppermute | solution.py:15
  511.0 15.8 %collective-permute-start.9 = (f32[1024,128]{1,0:T(8,128)}, f32[1024,128]{1,0:T(8,128)}, u32[]{:S(2)}, u32[]{:S(2)}) collective-permute-start(f32[1024,128]{1,0:T(8,128)} %scatter_custom_fusion.10), channel_id=1, source_target_pairs={{0,1},{1,2},{2,3},{3,4},{4,5},{5,6},{6,7},{7,8},{8,9},{9,10},{10,1... | collective-permute-start | bytes 1572872 | tf_op jit(solution)/shard_map/ppermute | solution.py:15
  530.9 115.4 %reduce-scatter.21.cloned.1.call-start = ((), (), s32[]{:S(2)}) async-start(), calls=%async_computation.20 | async-start | bytes 589824 | tf_op jit(solution)/shard_map/reduce_scatter | solution.py:55
  574.4 71.9 %copy-start.3 = (f32[128,128]{1,0:T(8,128)S(1)}, f32[128,128]{1,0:T(8,128)}, u32[]{:S(2)}) copy-start(f32[128,128]{1,0:T(8,128)} %reduce-scatter.17.cloned.1.call-done) | copy-start | bytes 196612
  574.4 16.0 %collective-permute-start.10 = (f32[1024,128]{1,0:T(8,128)}, f32[1024,128]{1,0:T(8,128)}, u32[]{:S(2)}, u32[]{:S(2)}) collective-permute-start(f32[1024,128]{1,0:T(8,128)} %bitcast.26), channel_id=1, source_target_pairs={{0,31},{1,0},{2,1},{3,2},{4,3},{5,4},{6,5},{7,6},{8,7},{9,8},{10,9... | collective-permute-start | bytes 1572872 | tf_op jit(solution)/shard_map/ppermute | solution.py:15
  598.8 16.2 %collective-permute-start.11 = (f32[1024,128]{1,0:T(8,128)}, f32[1024,128]{1,0:T(8,128)}, u32[]{:S(2)}, u32[]{:S(2)}) collective-permute-start(f32[1024,128]{1,0:T(8,128)} %scatter_custom_fusion.12), channel_id=1, source_target_pairs={{0,1},{1,2},{2,3},{3,4},{4,5},{5,6},{6,7},{7,8},{8,9},{9,10},{10,1... | collective-permute-start | bytes 1572872 | tf_op jit(solution)/shard_map/ppermute | solution.py:15
  619.0 186.7 %reduce-scatter.23.cloned.1.call-start = ((), (), s32[]{:S(2)}) async-start(), calls=%async_computation.21 | async-start | bytes 589824 | tf_op jit(solution)/shard_map/reduce_scatter | solution.py:55
  740.0 12.8 %collective-permute-start.12 = (f32[1024,128]{1,0:T(8,128)}, f32[1024,128]{1,0:T(8,128)}, u32[]{:S(2)}, u32[]{:S(2)}) collective-permute-start(f32[1024,128]{1,0:T(8,128)} %bitcast.28), channel_id=1, source_target_pairs={{0,31},{1,0},{2,1},{3,2},{4,3},{5,4},{6,5},{7,6},{8,7},{9,8},{10,9... | collective-permute-start | bytes 1572872 | tf_op jit(solution)/shard_map/ppermute | solution.py:15
  744.3 141.2 %copy-start.9 = (f32[128]{0:T(128)S(1)}, f32[128]{0:T(128)}, u32[]{:S(2)}) copy-start(f32[128]{0:T(128)} %copy-done.8) | copy-start | bytes 1540
  759.6 15.6 %collective-permute-start.13 = (f32[1024,128]{1,0:T(8,128)S(1)}, f32[1024,128]{1,0:T(8,128)S(1)}, u32[]{:S(2)}, u32[]{:S(2)}) collective-permute-start(f32[1024,128]{1,0:T(8,128)S(1)} %scatter_custom_fusion.14), channel_id=1, source_target_pairs={{0,1},{1,2},{2,3},{3,4},{4,5},{5,6},{6,7},{7,8},{8,9},{9,10},{10,1... | collective-permute-start | bytes 1572872 | tf_op jit(solution)/shard_map/ppermute | solution.py:15
  885.5 26.0 %copy-start.2 = (f32[128,128]{1,0:T(8,128)}, f32[128,128]{1,0:T(8,128)S(1)}, u32[]{:S(2)}) copy-start(f32[128,128]{1,0:T(8,128)S(1)} %get-tuple-element.13) | copy-start | bytes 196612
  898.3 12.4 %collective-permute-start.14 = (f32[1024,128]{1,0:T(8,128)S(1)}, f32[1024,128]{1,0:T(8,128)S(1)}, u32[]{:S(2)}, u32[]{:S(2)}) collective-permute-start(f32[1024,128]{1,0:T(8,128)S(1)} %bitcast.70), channel_id=1, source_target_pairs={{0,31},{1,0},{2,1},{3,2},{4,3},{5,4},{6,5},{7,6},{8,7},{9,8},{10,9... | collective-permute-start | bytes 1572872 | tf_op jit(solution)/shard_map/ppermute | solution.py:15
  (4 other events, 7.3 us)
Sparse Core Ops, SparseCore 0:
  61.3 31.2 reduce-scatter.24
  95.0 32.6 reduce-scatter.10
  194.1 27.0 reduce-scatter.12
  282.0 27.0 reduce-scatter.14
  368.8 27.0 reduce-scatter.16
  531.0 27.0 reduce-scatter.18
  619.2 27.0 reduce-scatter.20
  778.6 27.0 reduce-scatter.22
